TPU v7x, 32 devices: a whole 2x2x4 slice. The times are simulated.
32 devices in a mesh: grp: 4 (over y, core), row: 8 (over z, x).
Axes of the slice: x: 2, y: 2, z: 4, core: 2. Of those that a mesh axis runs over, the one named last changes fastest.
Arguments:
- grad: float32 [32, 2048, 512], P('grp', 'row')
- weight: bfloat16 [32, 2048, 512], P('grp', 'row'), may hold values from -0.125 to 0.125
- owner: int32 [32, 1], P('grp'), may hold values from 0 to 7; in each aligned block of 8 rows (0 to 7, 8 to 15, ...) at most 2 rows name the same one
- tokens: bfloat16 [3072, 2048], P('row'), may hold values from -6 to 6
- counts: int32 [8], P('row'), may hold values from 96 to 384, as said below
Outputs:
- new_weight: bfloat16 [32, 2048, 512], P('grp', 'row')
- mixed: bfloat16 [3072, 512], P('row', 'grp')
Inputs may be any that keep to these rules, and one draw needn't show every extreme that they name: Within each group's 8 consecutive matrices no owner is named more than 2 times, a bound that some block reaches. `counts`: some row index has all 384 rows live.
All inputs are finite; a program needn't handle non-finite values.
Results may differ from a plain program's by a relative error of at most 0.017.
Values may be sent and summed in bfloat16 or wider, within the bound.
A program may use at most 128 MiB of HBM per device.

v0:
```python
import jax
import jax.numpy as jnp
from jax import lax
from jax.sharding import PartitionSpec as P

ITERS = 5
MOST = 2
coef_a = 3.4445
coef_b = -4.775
coef_c = 2.0315
step_size = 0.5


def newton_schulz(start):
    iterate_state = start
    for turn in range(ITERS):
        gram_product = jnp.einsum(
            "jqz,jqa->jza", iterate_state, iterate_state, preferred_element_type=jnp.float32
        ).astype(jnp.bfloat16)
        square = jnp.einsum(
            "kfg,kgj->kfj", gram_product, gram_product, preferred_element_type=jnp.float32
        )
        polynomial_term = (coef_b * gram_product.astype(jnp.float32) + coef_c * square).astype(
            jnp.bfloat16
        )
        weight_update = jnp.einsum(
            "yon,ynb->yob", iterate_state, polynomial_term, preferred_element_type=jnp.float32
        )
        iterate_state = (coef_a * iterate_state.astype(jnp.float32) + weight_update).astype(
            jnp.bfloat16
        )
    return iterate_state


def body(grad, weight, owner, tokens, counts):
    ranks = lax.axis_size("row")
    groups = lax.axis_size("grp")
    number = grad.shape[0]
    rows = grad.shape[1]
    width = grad.shape[2]
    local = jnp.sum(grad * grad, axis=(1, 2))
    norm2 = lax.psum(local, "row")
    start = (grad / (jnp.sqrt(norm2) + 1e-07)[:, None, None]).astype(jnp.bfloat16)
    target = owner[:, 0]
    before = jnp.arange(number)[None, :] < jnp.arange(number)[:, None]
    same = target[None, :] == target[:, None]
    slot = jnp.sum((same & before).astype(jnp.int32), axis=1)
    place = target * MOST + slot
    table = (jnp.arange(ranks * MOST)[:, None] == place[None, :]).astype(jnp.bfloat16)

    def assemble(piece):
        count = piece.shape[1]
        return piece.transpose(1, 0, 2, 3).reshape(count, ranks * rows, width)

    ortho = newton_schulz(
        assemble(lax.all_to_all(start[:, None], "row", split_axis=0, concat_axis=0, tiled=True))
    )
    old = assemble(lax.all_to_all(weight[:, None], "row", split_axis=0, concat_axis=0, tiled=True))
    whole = (old.astype(jnp.float32) - step_size * ortho.astype(jnp.float32)).astype(jnp.bfloat16)
    count = whole.shape[0]
    solved = whole.reshape(count, ranks, rows, width).transpose(1, 0, 2, 3)
    returned_output = lax.all_to_all(solved, "row", split_axis=0, concat_axis=0, tiled=True)
    new_weight = returned_output[:, 0]
    moved = jnp.dot(
        table, new_weight.reshape(number, rows * width), preferred_element_type=jnp.float32
    )
    partial_output = jnp.einsum(
        "ix,oxv->iov",
        tokens,
        assemble(
            lax.all_to_all(
                moved.astype(jnp.bfloat16).reshape(ranks, MOST, rows, width),
                "row",
                split_axis=0,
                concat_axis=0,
                tiled=True,
            )
        ),
        preferred_element_type=jnp.float32,
    )
    proj = jnp.sum(partial_output, axis=1) * groups ** (-0.5)
    summed = lax.psum_scatter(
        proj.astype(jnp.bfloat16), "grp", scatter_dimension=1, tiled=True
    ).astype(jnp.float32)
    live = jnp.arange(summed.shape[0])[:, None] < counts[0]
    mixed = jnp.where(live, summed, 0.0).astype(jnp.bfloat16)
    return (new_weight, mixed)


def solution(mesh):
    placed = (
        P("grp", "row", None),
        P("grp", "row", None),
        P("grp", None),
        P("row", None),
        P("row"),
    )
    return jax.shard_map(
        body,
        mesh=mesh,
        in_specs=placed,
        out_specs=(P("grp", "row", None), P("row", "grp")),
        check_vma=False,
    )
```

profile of v0, /device:TPU:0, one launch (start us, length us, event | category | flops | bytes accessed | tf_op | source)
XLA Modules:
  0.0 347.3 jit_solution(1346113802811700175)
XLA Ops:
  7.2 0.0 copy-start
  7.2 2.7 multiply_reduce_fusion
  9.9 23.1 %psum.7 = f32[8]{0:T(128)S(1)} all-reduce(f32[8]{0:T(128)S(1)} %multiply_reduce_fusion), channel_id=1, replica_groups=mesh['grp'=4,'row'=8] {'row'}, use_global_device_ids=true, to_apply=%region_1.0 | all-reduce | flops 8 | bytes 64 | tf_op jit(solution)/shard_map/psum | solution.py:42
  33.0 2.8 fusion.3
  35.9 47.9 %all_to_all.20 = bf16[8,1,256,512]{3,2,1,0:T(8,128)(2,1)} all-to-all(bf16[8,1,256,512]{3,2,1,0:T(8,128)(2,1)S(1)} %fusion.3), channel_id=1, replica_groups=mesh['grp'=4,'row'=8] {'row'}, dimensions={0} | all-to-all | bytes 4194304 | tf_op jit(solution)/shard_map/all_to_all | solution.py:56
  83.8 4.3 %all-to-all-start = ((bf16[8,1,256,512]{3,2,1,0:T(8,128)(2,1)}), bf16[8,1,256,512]{3,2,1,0:T(8,128)(2,1)}, u32[]{:S(2)}, u32[]{:S(2)}) async-start(bf16[8,1,256,512]{3,2,1,0:T(8,128)(2,1)} %bitcast.74), calls=%async_computation | async-start | bytes 4194304 | tf_op jit(solution)/shard_map/all_to_all | solution.py:58
  88.2 3.5 %fusion.22 = bf16[512,512]{1,0:T(8,128)(2,1)S(1)} fusion(bf16[8,1,256,512]{3,2,1,0:T(8,128)(2,1)} %all_to_all.20), kind=kOutput, calls=%fused_computation.32 | convolution fusion | flops 1074003968 | bytes 2621440 | tf_op jit(solution)/shard_map/jqz,jqa->jza/dot_general | solution.py:17
  91.7 5.2 %add_convert_fusion.4 = bf16[2048,512]{1,0:T(8,128)(2,1)} fusion(bf16[2048,512]{1,0:T(8,128)(2,1)} %bitcast.76, bf16[512,512]{1,0:T(8,128)(2,1)S(1)} %fusion.22), kind=kOutput, calls=%fused_computation.7 | convolution fusion | flops 1347682304 | bytes 4718592 | tf_op jit(solution)/shard_map/yon,ynb->yob/dot_general | solution.py:26
  96.8 3.5 %convolution_convert_fusion.4 = bf16[512,512]{1,0:T(8,128)(2,1)S(1)} fusion(bf16[2048,512]{1,0:T(8,128)(2,1)} %add_convert_fusion.4), kind=kOutput, calls=%fused_computation.36 | convolution fusion | flops 1074003968 | bytes 2621440 | tf_op jit(solution)/shard_map/jqz,jqa->jza/dot_general | solution.py:17
  100.3 5.1 %add_convert_fusion.3 = bf16[2048,512]{1,0:T(8,128)(2,1)} fusion(bf16[2048,512]{1,0:T(8,128)(2,1)} %add_convert_fusion.4, bf16[512,512]{1,0:T(8,128)(2,1)S(1)} %convolution_convert_fusion.4), kind=kOutput, calls=%fused_computation.6 | convolution fusion | flops 1347682304 | bytes 4718592 | tf_op jit(solution)/shard_map/yon,ynb->yob/dot_general | solution.py:26
  105.5 3.5 %convolution_convert_fusion.3 = bf16[512,512]{1,0:T(8,128)(2,1)S(1)} fusion(bf16[2048,512]{1,0:T(8,128)(2,1)} %add_convert_fusion.3), kind=kOutput, calls=%fused_computation.35 | convolution fusion | flops 1074003968 | bytes 2621440 | tf_op jit(solution)/shard_map/jqz,jqa->jza/dot_general | solution.py:17
  109.0 5.2 %add_convert_fusion.2 = bf16[2048,512]{1,0:T(8,128)(2,1)} fusion(bf16[2048,512]{1,0:T(8,128)(2,1)} %add_convert_fusion.3, bf16[512,512]{1,0:T(8,128)(2,1)S(1)} %convolution_convert_fusion.3), kind=kOutput, calls=%fused_computation.5 | convolution fusion | flops 1347682304 | bytes 4718592 | tf_op jit(solution)/shard_map/yon,ynb->yob/dot_general | solution.py:26
  114.1 3.5 %convolution_convert_fusion.2 = bf16[512,512]{1,0:T(8,128)(2,1)S(1)} fusion(bf16[2048,512]{1,0:T(8,128)(2,1)} %add_convert_fusion.2), kind=kOutput, calls=%fused_computation.34 | convolution fusion | flops 1074003968 | bytes 2621440 | tf_op jit(solution)/shard_map/jqz,jqa->jza/dot_general | solution.py:17
  117.6 5.1 %add_convert_fusion.1 = bf16[2048,512]{1,0:T(8,128)(2,1)} fusion(bf16[2048,512]{1,0:T(8,128)(2,1)} %add_convert_fusion.2, bf16[512,512]{1,0:T(8,128)(2,1)S(1)} %convolution_convert_fusion.2), kind=kOutput, calls=%fused_computation.4 | convolution fusion | flops 1347682304 | bytes 4718592 | tf_op jit(solution)/shard_map/yon,ynb->yob/dot_general | solution.py:26
  122.8 3.5 %convolution_convert_fusion.1 = bf16[512,512]{1,0:T(8,128)(2,1)S(1)} fusion(bf16[2048,512]{1,0:T(8,128)(2,1)} %add_convert_fusion.1), kind=kOutput, calls=%fused_computation.33 | convolution fusion | flops 1074003968 | bytes 2621440 | tf_op jit(solution)/shard_map/jqz,jqa->jza/dot_general | solution.py:17
  126.2 8.5 %all-to-all-done = bf16[8,1,256,512]{3,2,1,0:T(8,128)(2,1)} async-done(((bf16[8,1,256,512]{3,2,1,0:T(8,128)(2,1)}), bf16[8,1,256,512]{3,2,1,0:T(8,128)(2,1)}, u32[]{:S(2)}, u32[]{:S(2)}) %all-to-all-start) | async-done | bytes 2097184 | tf_op jit(solution)/shard_map/all_to_all | solution.py:58
  134.8 5.6 %fusion = bf16[2048,512]{1,0:T(8,128)(2,1)} fusion(bf16[2048,512]{1,0:T(8,128)(2,1)} %bitcast.16, bf16[2048,512]{1,0:T(8,128)(2,1)} %add_convert_fusion.1, bf16[512,512]{1,0:T(8,128)(2,1)S(1)} %convolution_convert_fusion.1), kind=kOutput, calls=%fused_computation.2 | convolution fusion | flops 1352925184 | bytes 6815744 | tf_op jit(solution)/shard_map/yon,ynb->yob/dot_general | solution.py:26
  140.3 0.0 copy-start.1
  140.3 4.5 %all-to-all-start.2 = ((bf16[8,1,256,512]{3,2,1,0:T(8,128)(2,1)}), bf16[8,1,256,512]{3,2,1,0:T(8,128)(2,1)}, u32[]{:S(2)}, u32[]{:S(2)}) async-start(bf16[8,1,256,512]{3,2,1,0:T(8,128)(2,1)} %bitcast.75), calls=%async_computation.2 | async-start | bytes 4194304 | tf_op jit(solution)/shard_map/all_to_all | solution.py:62
  144.8 0.2 reduce-scatter.4.cloned.1.call-start
  145.1 0.0 copy-done.1
  145.1 0.2 convert_reduce_fusion
  145.3 47.2 %all-to-all-done.2 = bf16[8,1,256,512]{3,2,1,0:T(8,128)(2,1)} async-done(((bf16[8,1,256,512]{3,2,1,0:T(8,128)(2,1)}), bf16[8,1,256,512]{3,2,1,0:T(8,128)(2,1)}, u32[]{:S(2)}, u32[]{:S(2)}) %all-to-all-start.2) | async-done | bytes 2097184 | tf_op jit(solution)/shard_map/all_to_all | solution.py:62
  192.5 2.8 copy.20
  195.3 1.2 convolution_convert_fusion
  196.5 1.4 copy.21
  197.9 96.8 %all_to_all.21 = bf16[8,2,256,512]{3,2,1,0:T(8,128)(2,1)} all-to-all(bf16[8,2,256,512]{3,2,1,0:T(8,128)(2,1)S(1)} %bitcast.71), channel_id=1, replica_groups=mesh['grp'=4,'row'=8] {'row'}, dimensions={0} | all-to-all | bytes 8388608 | tf_op jit(solution)/shard_map/all_to_all | solution.py:71
  294.8 8.0 %copy.15 = bf16[2,8,256,512]{2,1,3,0:T(8,128)(2,1)} copy(bf16[2,8,256,512]{3,2,0,1:T(8,128)(2,1)} %bitcast.72) | data formatting | bytes 8388608 | tf_op jit(solution)/shard_map/transpose | solution.py:53
  302.7 7.4 %reshape.166 = bf16[2,2048,512]{1,2,0:T(8,128)(2,1)} reshape(bf16[2,8,256,512]{2,1,3,0:T(8,128)(2,1)} %copy.15) | data formatting | bytes 8388608 | tf_op jit(solution)/shard_map/reshape | solution.py:53
  310.1 0.0 copy-done
  310.1 4.6 %fusion.6 = f32[512,384]{1,0:T(8,128)S(1)} fusion(bf16[2,2048,512]{1,2,0:T(8,128)(2,1)} %reshape.166, bf16[384,2048]{1,0:T(8,128)(2,1)S(1)} %copy-done), kind=kOutput, calls=%fused_computation.15 | convolution fusion | flops 1610809344 | bytes 6553600 | tf_op jit(solution)/shard_map/ix,oxv->iov/dot_general | solution.py:67
  314.8 0.8 multiply_convert_fusion
  315.6 0.0 reduce-scatter.4.cloned.1.call-update
  316.3 19.4 %reduce-scatter.4.cloned.1.call-done = bf16[128,384]{1,0:T(8,128)(2,1)} async-done(((bf16[512,384]{1,0:T(8,128)(2,1)}), bf16[128,384]{1,0:T(8,128)(2,1)}) %reduce-scatter.4.cloned.1.call-update) | async-done | bytes 98320
  335.6 1.0 copy.19
  336.7 0.8 select_convert_fusion
  337.4 3.0 copy.24
  (3 shorter events, 0.0 us)
Async XLA Ops:
  7.2 303.0 %copy-start = (bf16[384,2048]{1,0:T(8,128)(2,1)S(1)}, bf16[384,2048]{1,0:T(8,128)(2,1)}, u32[]{:S(2)}) copy-start(bf16[384,2048]{1,0:T(8,128)(2,1)} %param.8) | copy-start | bytes 4718596
  83.8 51.0 %all-to-all-start = ((bf16[8,1,256,512]{3,2,1,0:T(8,128)(2,1)}), bf16[8,1,256,512]{3,2,1,0:T(8,128)(2,1)}, u32[]{:S(2)}, u32[]{:S(2)}) async-start(bf16[8,1,256,512]{3,2,1,0:T(8,128)(2,1)} %bitcast.74), calls=%async_computation | async-start | bytes 4194304 | tf_op jit(solution)/shard_map/all_to_all | solution.py:58
  140.3 4.7 %copy-start.1 = (s32[8,1]{0,1:T(1,128)S(1)}, s32[8,1]{0,1:T(1,128)}, u32[]{:S(2)}) copy-start(s32[8,1]{0,1:T(1,128)} %param.7) | copy-start | bytes 100
  140.3 52.2 %all-to-all-start.2 = ((bf16[8,1,256,512]{3,2,1,0:T(8,128)(2,1)}), bf16[8,1,256,512]{3,2,1,0:T(8,128)(2,1)}, u32[]{:S(2)}, u32[]{:S(2)}) async-start(bf16[8,1,256,512]{3,2,1,0:T(8,128)(2,1)} %bitcast.75), calls=%async_computation.2 | async-start | bytes 4194304 | tf_op jit(solution)/shard_map/all_to_all | solution.py:62
  144.8 190.8 %reduce-scatter.4.cloned.1.call-start = ((), (), s32[]{:S(2)}) async-start(), calls=%async_computation.5 | async-start | bytes 491520
Sparse Core Ops, SparseCore 0:
  315.7 19.8 reduce-scatter.3
where the time goes:
time: 348 us; the launch traced here: 347 us
  blocking collectives  168 us (48%)
  waiting for transfers between devices  75.2 us (22%)
  matrix products  49.4 us (14%)
  local copies, waits for them, and re-layouts  23.6 us (7%)
  between operations  14.8 us (4%)
  starting transfers between devices  9.05 us (3%)
  other arithmetic  7.35 us (2%)
    all_to_all x1, blocking collectives, body(): lax.all_to_all(moved.astype(jnp.bfloat16).reshape(ranks, MOST, rows, widt...  96.8 us
    all_to_all x1, blocking collectives, body(): lax.all_to_all(start[:, None], 'row', split_axis=0, concat_axis=0, tiled=...  47.9 us
    all_to_all x1, waiting for transfers between devices, body(): lax.all_to_all(solved, 'row', split_axis=0, concat_axis=0, tiled=True)  47.2 us
    dot_general x5, matrix products, newton_schulz(): jnp.einsum('yon,ynb->yob', iterate_state, polynomial_term, preferred_elem...  26.1 us
    psum x1, blocking collectives, body(): norm2 = lax.psum(local, 'row')  23.1 us
    unnamed x2, waiting for transfers between devices  19.4 us
    dot_general x5, matrix products, newton_schulz(): jnp.einsum('jqz,jqa->jza', iterate_state, iterate_state, preferred_elemen...  17.4 us
    all_to_all x1, waiting for transfers between devices, body(): lax.all_to_all(weight[:, None], 'row', split_axis=0, concat_axis=0, tiled...  8.54 us
  transfers between devices with their start and end apart: 3, of which 3 were waited for; matrix products, arithmetic and copies ran while one was open for 11% of the time, Pallas kernels for 0%

commit v1 on v0

--- a/solution.py
+++ b/solution.py
@@ -39,7 +39,9 @@
     rows = grad.shape[1]
     width = grad.shape[2]
     local = jnp.sum(grad * grad, axis=(1, 2))
-    norm2 = lax.psum(local, "row")
+    norm2 = local
+    for hop in (1, 2, 4):
+        norm2 = norm2 + lax.ppermute(norm2, "row", [(dev, dev ^ hop) for dev in range(8)])
     start = (grad / (jnp.sqrt(norm2) + 1e-07)[:, None, None]).astype(jnp.bfloat16)
     target = owner[:, 0]
     before = jnp.arange(number)[None, :] < jnp.arange(number)[:, None]

time: 348 us -> 339 us (0.974)
  blocking collectives: 168 us -> 148 us
  starting transfers between devices: 9.05 us -> 17.2 us
  waiting for transfers between devices: 75.2 us -> 79.8 us
    psum x1 -> x0, blocking collectives: 23.1 us -> none  [body(): norm2 = lax.psum(local, 'row')]
    ppermute x0 -> x3, starting transfers between devices: none -> 8.11 us  [body(): lax.ppermute(norm2, 'row', [(dev, dev ^ hop) for dev in range(8)])]
    ppermute x0 -> x3, waiting for transfers between devices: none -> 4.64 us  [body(): lax.ppermute(norm2, 'row', [(dev, dev ^ hop) for dev in range(8)])]
    unnamed x8 -> x10, local copies, waits for them, and re-layouts: 8.25 us -> 8.26 us
  transfers between devices with their start and end apart: 3 -> 6, of which waited for: 3 -> 6; matrix products, arithmetic and copies ran while one was open for 11% -> 11% of each run, Pallas kernels for 0% -> 0%
where the time goes in v1:
time: 339 us; the launch traced here: 338 us
  blocking collectives  148 us (44%)
  waiting for transfers between devices  79.8 us (24%)
  matrix products  49.5 us (15%)
  local copies, waits for them, and re-layouts  23.6 us (7%)
  starting transfers between devices  17.2 us (5%)
  between operations  14.8 us (4%)
  other arithmetic  5.19 us (2%)
    all_to_all x1, blocking collectives, body(): lax.all_to_all(moved.astype(jnp.bfloat16).reshape(ranks, MOST, rows, widt...  96.9 us
    all_to_all x1, blocking collectives, body(): lax.all_to_all(start[:, None], 'row', split_axis=0, concat_axis=0, tiled=...  50.8 us
    all_to_all x1, waiting for transfers between devices, body(): lax.all_to_all(solved, 'row', split_axis=0, concat_axis=0, tiled=True)  47.2 us
    dot_general x5, matrix products, newton_schulz(): jnp.einsum('yon,ynb->yob', iterate_state, polynomial_term, preferred_elem...  26.2 us
    unnamed x2, waiting for transfers between devices  19.4 us
    dot_general x5, matrix products, newton_schulz(): jnp.einsum('jqz,jqa->jza', iterate_state, iterate_state, preferred_elemen...  17.4 us
    all_to_all x1, waiting for transfers between devices, body(): lax.all_to_all(weight[:, None], 'row', split_axis=0, concat_axis=0, tiled...  8.53 us
    unnamed x10, local copies, waits for them, and re-layouts  8.26 us
  transfers between devices with their start and end apart: 6, of which 6 were waited for; matrix products, arithmetic and copies ran while one was open for 11% of the time, Pallas kernels for 0%

profile of v1, /device:TPU:0, one launch (start us, length us, event | category | flops | bytes accessed | tf_op | source)
XLA Modules:
  0.0 337.7 jit_solution(3391774152664892281)
XLA Ops:
  7.2 0.0 copy-start
  7.2 0.0 copy-start.1
  7.2 2.8 multiply_reduce_fusion
  10.0 3.0 collective-permute-start
  12.9 1.5 collective-permute-done
  14.5 2.1 collective-permute-start.1
  16.6 1.5 collective-permute-done.1
  18.1 3.0 collective-permute-start.2
  21.2 1.5 collective-permute-done.2
  22.7 0.0 copy-done.1
  22.7 0.6 fusion.3
  23.4 50.8 %all_to_all.20 = bf16[8,1,256,512]{3,2,1,0:T(8,128)(2,1)} all-to-all(bf16[8,1,256,512]{3,2,1,0:T(8,128)(2,1)S(1)} %fusion.3), channel_id=1, replica_groups=mesh['grp'=4,'row'=8] {'row'}, dimensions={0} | all-to-all | bytes 4194304 | tf_op jit(solution)/shard_map/all_to_all | solution.py:58
  74.2 4.3 %all-to-all-start = ((bf16[8,1,256,512]{3,2,1,0:T(8,128)(2,1)}), bf16[8,1,256,512]{3,2,1,0:T(8,128)(2,1)}, u32[]{:S(2)}, u32[]{:S(2)}) async-start(bf16[8,1,256,512]{3,2,1,0:T(8,128)(2,1)} %bitcast.74), calls=%async_computation | async-start | bytes 4194304 | tf_op jit(solution)/shard_map/all_to_all | solution.py:60
  78.6 3.5 %fusion.22 = bf16[512,512]{1,0:T(8,128)(2,1)S(1)} fusion(bf16[8,1,256,512]{3,2,1,0:T(8,128)(2,1)} %all_to_all.20), kind=kOutput, calls=%fused_computation.32 | convolution fusion | flops 1074003968 | bytes 2621440 | tf_op jit(solution)/shard_map/jqz,jqa->jza/dot_general | solution.py:17
  82.1 5.2 %add_convert_fusion.4 = bf16[2048,512]{1,0:T(8,128)(2,1)} fusion(bf16[2048,512]{1,0:T(8,128)(2,1)} %bitcast.76, bf16[512,512]{1,0:T(8,128)(2,1)S(1)} %fusion.22), kind=kOutput, calls=%fused_computation.7 | convolution fusion | flops 1347682304 | bytes 4718592 | tf_op jit(solution)/shard_map/yon,ynb->yob/dot_general | solution.py:26
  87.2 3.5 %convolution_convert_fusion.4 = bf16[512,512]{1,0:T(8,128)(2,1)S(1)} fusion(bf16[2048,512]{1,0:T(8,128)(2,1)} %add_convert_fusion.4), kind=kOutput, calls=%fused_computation.36 | convolution fusion | flops 1074003968 | bytes 2621440 | tf_op jit(solution)/shard_map/jqz,jqa->jza/dot_general | solution.py:17
  90.7 5.1 %add_convert_fusion.3 = bf16[2048,512]{1,0:T(8,128)(2,1)} fusion(bf16[2048,512]{1,0:T(8,128)(2,1)} %add_convert_fusion.4, bf16[512,512]{1,0:T(8,128)(2,1)S(1)} %convolution_convert_fusion.4), kind=kOutput, calls=%fused_computation.6 | convolution fusion | flops 1347682304 | bytes 4718592 | tf_op jit(solution)/shard_map/yon,ynb->yob/dot_general | solution.py:26
  95.9 3.5 %convolution_convert_fusion.3 = bf16[512,512]{1,0:T(8,128)(2,1)S(1)} fusion(bf16[2048,512]{1,0:T(8,128)(2,1)} %add_convert_fusion.3), kind=kOutput, calls=%fused_computation.35 | convolution fusion | flops 1074003968 | bytes 2621440 | tf_op jit(solution)/shard_map/jqz,jqa->jza/dot_general | solution.py:17
  99.4 5.2 %add_convert_fusion.2 = bf16[2048,512]{1,0:T(8,128)(2,1)} fusion(bf16[2048,512]{1,0:T(8,128)(2,1)} %add_convert_fusion.3, bf16[512,512]{1,0:T(8,128)(2,1)S(1)} %convolution_convert_fusion.3), kind=kOutput, calls=%fused_computation.5 | convolution fusion | flops 1347682304 | bytes 4718592 | tf_op jit(solution)/shard_map/yon,ynb->yob/dot_general | solution.py:26
  104.5 3.5 %convolution_convert_fusion.2 = bf16[512,512]{1,0:T(8,128)(2,1)S(1)} fusion(bf16[2048,512]{1,0:T(8,128)(2,1)} %add_convert_fusion.2), kind=kOutput, calls=%fused_computation.34 | convolution fusion | flops 1074003968 | bytes 2621440 | tf_op jit(solution)/shard_map/jqz,jqa->jza/dot_general | solution.py:17
  108.0 5.1 %add_convert_fusion.1 = bf16[2048,512]{1,0:T(8,128)(2,1)} fusion(bf16[2048,512]{1,0:T(8,128)(2,1)} %add_convert_fusion.2, bf16[512,512]{1,0:T(8,128)(2,1)S(1)} %convolution_convert_fusion.2), kind=kOutput, calls=%fused_computation.4 | convolution fusion | flops 1347682304 | bytes 4718592 | tf_op jit(solution)/shard_map/yon,ynb->yob/dot_general | solution.py:26
  113.2 3.5 %convolution_convert_fusion.1 = bf16[512,512]{1,0:T(8,128)(2,1)S(1)} fusion(bf16[2048,512]{1,0:T(8,128)(2,1)} %add_convert_fusion.1), kind=kOutput, calls=%fused_computation.33 | convolution fusion | flops 1074003968 | bytes 2621440 | tf_op jit(solution)/shard_map/jqz,jqa->jza/dot_general | solution.py:17
  116.7 8.5 %all-to-all-done = bf16[8,1,256,512]{3,2,1,0:T(8,128)(2,1)} async-done(((bf16[8,1,256,512]{3,2,1,0:T(8,128)(2,1)}), bf16[8,1,256,512]{3,2,1,0:T(8,128)(2,1)}, u32[]{:S(2)}, u32[]{:S(2)}) %all-to-all-start) | async-done | bytes 2097184 | tf_op jit(solution)/shard_map/all_to_all | solution.py:60
  125.2 5.6 %fusion = bf16[2048,512]{1,0:T(8,128)(2,1)} fusion(bf16[2048,512]{1,0:T(8,128)(2,1)} %bitcast.16, bf16[2048,512]{1,0:T(8,128)(2,1)} %add_convert_fusion.1, bf16[512,512]{1,0:T(8,128)(2,1)S(1)} %convolution_convert_fusion.1), kind=kOutput, calls=%fused_computation.2 | convolution fusion | flops 1352925184 | bytes 6815744 | tf_op jit(solution)/shard_map/yon,ynb->yob/dot_general | solution.py:26
  130.7 0.0 copy-start.2
  130.7 4.7 %all-to-all-start.2 = ((bf16[8,1,256,512]{3,2,1,0:T(8,128)(2,1)}), bf16[8,1,256,512]{3,2,1,0:T(8,128)(2,1)}, u32[]{:S(2)}, u32[]{:S(2)}) async-start(bf16[8,1,256,512]{3,2,1,0:T(8,128)(2,1)} %bitcast.75), calls=%async_computation.2 | async-start | bytes 4194304 | tf_op jit(solution)/shard_map/all_to_all | solution.py:64
  135.4 0.0 reduce-scatter.4.cloned.1.call-start
  135.5 0.0 copy-done.2
  135.5 0.2 convert_reduce_fusion
  135.7 47.2 %all-to-all-done.2 = bf16[8,1,256,512]{3,2,1,0:T(8,128)(2,1)} async-done(((bf16[8,1,256,512]{3,2,1,0:T(8,128)(2,1)}), bf16[8,1,256,512]{3,2,1,0:T(8,128)(2,1)}, u32[]{:S(2)}, u32[]{:S(2)}) %all-to-all-start.2) | async-done | bytes 2097184 | tf_op jit(solution)/shard_map/all_to_all | solution.py:64
  182.9 2.8 copy.20
  185.6 1.2 convolution_convert_fusion
  186.9 1.4 copy.21
  188.3 96.9 %all_to_all.21 = bf16[8,2,256,512]{3,2,1,0:T(8,128)(2,1)} all-to-all(bf16[8,2,256,512]{3,2,1,0:T(8,128)(2,1)S(1)} %bitcast.71), channel_id=1, replica_groups=mesh['grp'=4,'row'=8] {'row'}, dimensions={0} | all-to-all | bytes 8388608 | tf_op jit(solution)/shard_map/all_to_all | solution.py:73
  285.2 8.0 %copy.15 = bf16[2,8,256,512]{2,1,3,0:T(8,128)(2,1)} copy(bf16[2,8,256,512]{3,2,0,1:T(8,128)(2,1)} %bitcast.72) | data formatting | bytes 8388608 | tf_op jit(solution)/shard_map/transpose | solution.py:55
  293.1 7.4 %reshape.166 = bf16[2,2048,512]{1,2,0:T(8,128)(2,1)} reshape(bf16[2,8,256,512]{2,1,3,0:T(8,128)(2,1)} %copy.15) | data formatting | bytes 8388608 | tf_op jit(solution)/shard_map/reshape | solution.py:55
  300.5 0.0 copy-done
  300.5 4.6 %fusion.6 = f32[512,384]{1,0:T(8,128)S(1)} fusion(bf16[2,2048,512]{1,2,0:T(8,128)(2,1)} %reshape.166, bf16[384,2048]{1,0:T(8,128)(2,1)S(1)} %copy-done), kind=kOutput, calls=%fused_computation.15 | convolution fusion | flops 1610809344 | bytes 6553600 | tf_op jit(solution)/shard_map/ix,oxv->iov/dot_general | solution.py:69
  305.2 0.8 multiply_convert_fusion
  306.0 0.0 reduce-scatter.4.cloned.1.call-update
  306.7 19.4 %reduce-scatter.4.cloned.1.call-done = bf16[128,384]{1,0:T(8,128)(2,1)} async-done(((bf16[512,384]{1,0:T(8,128)(2,1)}), bf16[128,384]{1,0:T(8,128)(2,1)}) %reduce-scatter.4.cloned.1.call-update) | async-done | bytes 98320
  326.0 1.0 copy.19
  327.1 0.8 select_convert_fusion
  327.8 3.0 copy.24
  (5 shorter events, 0.0 us)
Async XLA Ops:
  7.2 293.4 %copy-start = (bf16[384,2048]{1,0:T(8,128)(2,1)S(1)}, bf16[384,2048]{1,0:T(8,128)(2,1)}, u32[]{:S(2)}) copy-start(bf16[384,2048]{1,0:T(8,128)(2,1)} %param.8) | copy-start | bytes 4718596
  7.2 15.6 %copy-start.1 = (f32[8,256,512]{2,1,0:T(8,128)S(1)}, f32[8,256,512]{2,1,0:T(8,128)}, u32[]{:S(2)}) copy-start(f32[8,256,512]{2,1,0:T(8,128)} %param.5) | copy-start | bytes 12582916
  10.0 4.5 %collective-permute-start = (f32[8]{0:T(128)S(1)}, f32[8]{0:T(128)S(1)}, u32[]{:S(2)}, u32[]{:S(2)}) collective-permute-start(f32[8]{0:T(128)S(1)} %multiply_reduce_fusion), channel_id=1, source_target_pairs={{0,1},{1,0},{2,3},{3,2},{4,5},{5,4},{6,7},{7,6},{8,9},{9,8},{10,11... | collective-permute-start | bytes 104 | tf_op jit(solution)/shard_map/ppermute | solution.py:44
  14.5 3.7 %collective-permute-start.1 = (f32[8]{0:T(128)S(1)}, f32[8]{0:T(128)S(1)}, u32[]{:S(2)}, u32[]{:S(2)}) collective-permute-start(f32[8]{0:T(128)S(1)} %add.61), channel_id=1, source_target_pairs={{0,2},{1,3},{2,0},{3,1},{4,6},{5,7},{6,4},{7,5},{8,10},{9,11},{10,... | collective-permute-start | bytes 104 | tf_op jit(solution)/shard_map/ppermute | solution.py:44
  18.1 4.6 %collective-permute-start.2 = (f32[8]{0:T(128)S(1)}, f32[8]{0:T(128)S(1)}, u32[]{:S(2)}, u32[]{:S(2)}) collective-permute-start(f32[8]{0:T(128)S(1)} %add.62), channel_id=1, source_target_pairs={{0,4},{1,5},{2,6},{3,7},{4,0},{5,1},{6,2},{7,3},{8,12},{9,13},{10,... | collective-permute-start | bytes 104 | tf_op jit(solution)/shard_map/ppermute | solution.py:44
  74.2 51.0 %all-to-all-start = ((bf16[8,1,256,512]{3,2,1,0:T(8,128)(2,1)}), bf16[8,1,256,512]{3,2,1,0:T(8,128)(2,1)}, u32[]{:S(2)}, u32[]{:S(2)}) async-start(bf16[8,1,256,512]{3,2,1,0:T(8,128)(2,1)} %bitcast.74), calls=%async_computation | async-start | bytes 4194304 | tf_op jit(solution)/shard_map/all_to_all | solution.py:60
  130.7 4.7 %copy-start.2 = (s32[8,1]{0,1:T(1,128)S(1)}, s32[8,1]{0,1:T(1,128)}, u32[]{:S(2)}) copy-start(s32[8,1]{0,1:T(1,128)} %param.7) | copy-start | bytes 100
  130.7 52.1 %all-to-all-start.2 = ((bf16[8,1,256,512]{3,2,1,0:T(8,128)(2,1)}), bf16[8,1,256,512]{3,2,1,0:T(8,128)(2,1)}, u32[]{:S(2)}, u32[]{:S(2)}) async-start(bf16[8,1,256,512]{3,2,1,0:T(8,128)(2,1)} %bitcast.75), calls=%async_computation.2 | async-start | bytes 4194304 | tf_op jit(solution)/shard_map/all_to_all | solution.py:64
  135.4 190.6 %reduce-scatter.4.cloned.1.call-start = ((), (), s32[]{:S(2)}) async-start(), calls=%async_computation.5 | async-start | bytes 491520
Sparse Core Ops, SparseCore 0:
  306.1 19.8 reduce-scatter.3
